TPU v7x, 32 devices: a whole 2x2x4 slice. The times are simulated.
32 devices in a mesh: grp: 2 (over x), row: 16 (over z, y, core).
Axes of the slice: x: 2, y: 2, z: 4, core: 2. Of those that a mesh axis runs over, the one named last changes fastest.
Arguments:
- field: bfloat16 [256, 1024, 256], P(('grp', 'row')), parts along dimension 0, may hold values from -8 to 8, as said below
- w_qkv: bfloat16 [256, 768], replicated, may hold values from -0.375 to 0.375
- w_attn: bfloat16 [256, 256], replicated, may hold values from -0.375 to 0.375
- w_inner: bfloat16 [256, 512], replicated, may hold values from -0.375 to 0.375
- w_outer: bfloat16 [512, 256], replicated, may hold values from -0.25 to 0.25
- w_skip: bfloat16 [256, 256], replicated, may hold values from -0.375 to 0.375
- w_modes: bfloat16 [512, 2, 256, 256], P('row'), may hold values from -0.25 to 0.25
Outputs:
- result: bfloat16 [256, 1024, 256], P(('grp', 'row')), parts along dimension 0
There are 2 independent parts, one for each index of `grp`. A program takes and returns all parts, laid end to end along the dimension named above; an argument that names none is the same for every part. Nothing has to cross between parts.
Inputs may be any that keep to these rules, and one draw needn't show every extreme that they name: `field`: features of the slab's cells.
All inputs are finite; a program needn't handle non-finite values.
Results may differ from a plain program's by a relative error of at most 0.004.
The roundings to bfloat16 on the way count: a program that leaves them out, or rounds other values in their place, can miss the bound.
Values may be sent and summed in bfloat16 or wider, within the bound.
No kernel may reach another device: no remote copies, remote signals or barrier semaphores. Data moves between devices by JAX's collectives and lax.ppermute only.
A program may use at most 128 MiB of HBM per device.

v0:
```python
import jax
import jax.numpy as jnp
from jax import lax
from jax.sharding import PartitionSpec as P

HEADS = 4
HD = 64
MH = 32
MW = 16
EPSILON = 1e-05
TWO_PI = 6.283185307179586


def head_norm(blocked, heads):
    shaped = blocked.reshape(blocked.shape[0], heads, -1)
    center = shaped - jnp.mean(shaped, axis=-1, keepdims=True)
    spread = jnp.mean(center * center, axis=-1, keepdims=True)
    return (center * lax.rsqrt(spread + EPSILON)).astype(jnp.bfloat16)


def column_table(columns, modes):
    col_index = jnp.arange(columns, dtype=jnp.int32)
    freqs = jnp.arange(modes, dtype=jnp.int32)
    turns = freqs[:, None] * col_index[None, :] % columns
    angle = turns.astype(jnp.float32) * (TWO_PI / columns)
    return (jnp.cos(angle), jnp.sin(angle))


def row_angles(height, modes, rows_global):
    freqs = jnp.arange(modes, dtype=jnp.int32)
    signed = jnp.where(freqs < modes // 2, freqs, freqs - modes + height)
    turns = signed[:, None] * rows_global[None, :] % height
    angle = turns.astype(jnp.float32) * (TWO_PI / height)
    return (jnp.cos(angle), jnp.sin(angle))


def local(field, w_qkv, w_attn, w_inner, w_outer, w_skip, w_modes):
    strip_rows, columns, channels = field.shape
    highest = lax.Precision.HIGHEST
    height = strip_rows * lax.axis_size("row")
    rows_global = lax.axis_index("row") * strip_rows + jnp.arange(strip_rows, dtype=jnp.int32)
    tokens = field.reshape(-1, channels)
    projected = jnp.dot(tokens, w_qkv, preferred_element_type=jnp.float32)
    queries = projected[:, :channels].astype(jnp.bfloat16).reshape(-1, HEADS, HD)
    key_rows = head_norm(projected[:, channels : 2 * channels], HEADS)
    value_rows = head_norm(projected[:, 2 * channels :], HEADS)
    partial_kv = jnp.einsum(
        "thd,the->hde", key_rows, value_rows, preferred_element_type=jnp.float32
    )
    summed_kv = lax.psum(partial_kv, "row")
    scaled_kv = (summed_kv / (height * columns)).astype(jnp.bfloat16)
    attended = jnp.einsum("thd,hde->the", queries, scaled_kv, preferred_element_type=jnp.float32)
    attended = attended.astype(jnp.bfloat16).reshape(-1, channels)
    first = (
        tokens.astype(jnp.float32) + jnp.dot(attended, w_attn, preferred_element_type=jnp.float32)
    ).astype(jnp.bfloat16)
    hidden = jax.nn.gelu(
        jnp.dot(first, w_inner, preferred_element_type=jnp.float32), approximate=False
    ).astype(jnp.bfloat16)
    second = (
        first.astype(jnp.float32) + jnp.dot(hidden, w_outer, preferred_element_type=jnp.float32)
    ).astype(jnp.bfloat16)
    slab_grid = second.reshape(strip_rows, columns, channels)
    col_cos, col_sin = column_table(columns, MW)
    forward_tab = jnp.concatenate([col_cos, -col_sin], axis=0).T.astype(jnp.bfloat16)
    row_spectra = jnp.einsum(
        "rwc,wk->rkc", slab_grid, forward_tab, preferred_element_type=jnp.float32
    )
    spec_re = row_spectra[:, :MW]
    spec_im = row_spectra[:, MW:]
    row_cos, row_sin = row_angles(height, MH, rows_global)
    coeff_re = jnp.einsum("hr,rkc->hkc", row_cos, spec_re, precision=highest) + jnp.einsum(
        "hr,rkc->hkc", row_sin, spec_im, precision=highest
    )
    coeff_im = jnp.einsum("hr,rkc->hkc", row_cos, spec_im, precision=highest) - jnp.einsum(
        "hr,rkc->hkc", row_sin, spec_re, precision=highest
    )
    term_modes = jnp.concatenate([coeff_re, coeff_im], axis=-1).reshape(MH * MW, 2 * channels)
    owned = lax.psum_scatter(term_modes, "row", scatter_dimension=0, tiled=True)
    owned_b = owned.astype(jnp.bfloat16)
    part_re = owned_b[:, :channels]
    part_im = owned_b[:, channels:]
    mode_re = w_modes[:, 0]
    mode_im = w_modes[:, 1]
    mixed_re = jnp.einsum(
        "mc,mco->mo", part_re, mode_re, preferred_element_type=jnp.float32
    ) - jnp.einsum("mc,mco->mo", part_im, mode_im, preferred_element_type=jnp.float32)
    mixed_im = jnp.einsum(
        "mc,mco->mo", part_re, mode_im, preferred_element_type=jnp.float32
    ) + jnp.einsum("mc,mco->mo", part_im, mode_re, preferred_element_type=jnp.float32)
    mixed = jnp.concatenate([mixed_re, mixed_im], axis=-1).astype(jnp.bfloat16)
    segment = lax.all_gather(mixed, "row", axis=0, tiled=True)
    seg_count = segment.shape[0]
    mode_index = jnp.arange(seg_count, dtype=jnp.int32)
    mode_row = mode_index // MW
    mode_col = mode_index % MW
    signed = jnp.where(mode_row < MH // 2, mode_row, mode_row - MH + height)
    turns = signed[:, None] * rows_global[None, :] % height
    angle = turns.astype(jnp.float32) * (TWO_PI / height)
    seg_cos = jnp.cos(angle)[:, :, None]
    seg_sin = jnp.sin(angle)[:, :, None]
    seg_f = segment.astype(jnp.float32)
    seg_re = seg_f[:, None, :channels]
    seg_im = seg_f[:, None, channels:]
    turned = jnp.concatenate(
        [seg_cos * seg_re - seg_sin * seg_im, seg_cos * seg_im + seg_sin * seg_re], axis=-1
    )
    select = (mode_col[:, None] == jnp.arange(MW, dtype=jnp.int32)[None, :]).astype(jnp.float32)
    back_sum = jnp.einsum("mk,mrc->rkc", select, turned, precision=highest)
    weights_kw = jnp.where(jnp.arange(MW, dtype=jnp.int32) == 0, 1.0, 2.0).astype(jnp.float32) / (
        height * columns
    )
    back = (back_sum * weights_kw[None, :, None]).astype(jnp.bfloat16)
    back_stack = jnp.concatenate([back[..., :channels], back[..., channels:]], axis=1)
    inverse_tab = jnp.concatenate([col_cos, -col_sin], axis=0).astype(jnp.bfloat16)
    spectral = jnp.einsum(
        "rkc,kw->rwc", back_stack, inverse_tab, preferred_element_type=jnp.float32
    )
    skipped = jnp.dot(second, w_skip, preferred_element_type=jnp.float32)
    result = jax.nn.gelu(skipped + spectral.reshape(-1, channels), approximate=False)
    return result.astype(jnp.bfloat16).reshape(strip_rows, columns, channels)


def solution(mesh):
    placed = (P(("grp", "row"), None, None), P(), P(), P(), P(), P(), P("row", None, None, None))
    return jax.shard_map(
        local, mesh=mesh, in_specs=placed, out_specs=P(("grp", "row"), None, None), check_vma=False
    )
```

profile of v0, /device:TPU:0, one launch (start us, length us, event | category | flops | bytes accessed | tf_op | source)
XLA Modules:
  0.0 315.8 jit_solution(15945450065870714248)
XLA Ops:
  6.5 1.0 copy-done
  7.5 12.3 %fusion.165 = f32[8192,768]{0,1:T(8,128)} fusion(bf16[8192,256]{1,0:T(8,128)(2,1)} %bitcast.87, bf16[256,768]{1,0:T(8,128)(2,1)S(1)} %copy-done), kind=kOutput, calls=%fused_computation.221 | convolution fusion | flops 3221225472 | bytes 29753344 | tf_op jit(solution)/shard_map/dot_general | solution.py:43
  19.8 6.6 %bitcast_reduce_fusion.1 = (f32[8192,4]{0,1:T(4,128)S(1)}, f32[8192,4]{0,1:T(4,128)S(1)}) fusion(f32[8192,768]{0,1:T(8,128)} %fusion.165), kind=kLoop, calls=%fused_computation.37 | loop fusion | flops 4128768 | bytes 17039360 | tf_op jit(solution)/shard_map/reduce_sum | solution.py:16
  26.4 7.2 %multiply_reduce_fusion.1 = (f32[8192,4]{0,1:T(4,128)S(1)}, f32[8192,4]{0,1:T(4,128)S(1)}) fusion(f32[8192,768]{0,1:T(8,128)} %fusion.165, f32[8192,4]{0,1:T(4,128)S(1)} %get-tuple-element.22, f32[8192,4]{0,1:T(4,128)S(1)} %get-tuple-element.21), kind=kLoop, calls=%fused_computation.54 | loop fusion | flops 12517376 | bytes 17301504 | tf_op jit(solution)/shard_map/reduce_sum | solution.py:17
  33.7 8.0 %fusion.29 = f32[4,64,64]{1,2,0:T(8,128)} fusion(f32[8192,768]{0,1:T(8,128)} %fusion.165, f32[8192,4]{0,1:T(4,128)S(1)} %add_rsqrt_fusion, f32[8192,4]{0,1:T(4,128)S(1)} %get-tuple-element.21, f32[8192,4]{0,1:T(4,128)S(1)} %add_rsqrt_fusion.1, f32[8192,4]{0,1:T(4,128)S(1)} %get-tuple-element.22), kind=kOutput, calls=%fused_computation.58 | convolution fusion | flops 281018368 | bytes 17367040 | tf_op jit(solution)/shard_map/thd,the->hde/dot_general | solution.py:47
  41.8 0.9 sine_negate_fusion
  43.8 6.0 %slice.91 = bf16[8192,256]{0,1:T(8,128)(2,1)} slice(f32[8192,768]{0,1:T(8,128)} %fusion.165), slice={[0:8192], [0:256]} | slice | bytes 8388608 | tf_op jit(solution)/shard_map/slice | solution.py:44
  49.8 83.0 %all-reduce.2.cloned.1.call-done = f32[4,64,64]{1,2,0:T(8,128)} async-done(((f32[4,64,64]{1,2,0:T(8,128)}), f32[4,64,64]{1,2,0:T(8,128)}) %all-reduce.2.cloned.1.call-update) | async-done | bytes 65552 | tf_op jit(solution)/shard_map/psum | solution.py:50
  132.8 3.6 %convolution_convert_fusion = bf16[4,64,8192]{2,1,0:T(8,128)(2,1)S(1)} fusion(bf16[8192,4,64]{0,2,1:T(8,128)(2,1)} %bitcast.86, f32[4,64,64]{1,2,0:T(8,128)} %all-reduce.2.cloned.1.call-done), kind=kOutput, calls=%fused_computation.22 | convolution fusion | flops 270565376 | bytes 8454144 | tf_op jit(solution)/shard_map/thd,hde->the/dot_general | solution.py:52
  136.5 3.3 %fusion.10 = bf16[8192,256]{1,0:T(8,128)(2,1)} fusion(bf16[8192,256]{0,1:T(8,128)(2,1)S(1)} %bitcast.85, bf16[256,256]{1,0:T(8,128)(2,1)S(1)} %copy-done.6, bf16[8192,256]{1,0:T(8,128)(2,1)S(1)} %bitcast.88), kind=kOutput, calls=%fused_computation.23 | convolution fusion | flops 1080033280 | bytes 12713984 | tf_op jit(solution)/shard_map/dot_general | solution.py:55
  139.9 42.3 %fusion.11 = bf16[8192,256]{1,0:T(8,128)(2,1)} fusion(bf16[512,256]{1,0:T(8,128)(2,1)S(1)} %copy-done.9, bf16[8192,256]{1,0:T(8,128)(2,1)} %fusion.10, bf16[256,512]{1,0:T(8,128)(2,1)S(1)} %copy-done.10), kind=kOutput, calls=%fused_computation.25 | convolution fusion | flops 4573888512 | bytes 8912896 | tf_op jit(solution)/shard_map/dot_general | solution.py:61
  182.2 3.0 convolution_bitcast_fusion
  188.4 1.6 copy.16
  190.2 59.1 %reduce-scatter.2.cloned.1.call-done = f32[32,512]{1,0:T(8,128)} async-done(((f32[512,512]{1,0:T(8,128)}), f32[32,512]{1,0:T(8,128)}) %reduce-scatter.2.cloned.1.call-update) | async-done | bytes 65552 | tf_op jit(solution)/shard_map/reduce_scatter | solution.py:79
  249.3 0.8 convert_element_type.85
  250.1 2.8 fusion.36
  253.0 2.8 fusion.30
  255.8 2.8 fusion.32
  258.6 2.8 fusion.34
  261.5 20.9 %all_gather.3 = bf16[512,512]{1,0:T(8,128)(2,1)S(1)} all-gather(bf16[32,512]{1,0:T(8,128)(2,1)S(1)} %pad_maximum_fusion.1), channel_id=1, replica_groups=mesh['grp'=2,'row'=16] {'row'}, dimensions={0}, use_global_device_ids=true | all-gather | bytes 557056 | tf_op jit(solution)/shard_map/all_gather | solution.py:92
  282.5 1.3 multiply_subtract_fusion
  283.8 2.8 fusion.52
  286.6 1.3 fusion.55
  287.9 21.0 %fusion.14 = bf16[8192,256]{1,0:T(8,128)(2,1)} fusion(f32[8192,256]{1,0:T(8,128)S(1)} %bitcast.89, bf16[8192,256]{1,0:T(8,128)(2,1)S(1)} %copy-done.3, bf16[256,256]{1,0:T(8,128)(2,1)S(1)} %copy-done.11), kind=kOutput, calls=%fused_computation.28 | convolution fusion | flops 1212153856 | bytes 16908288 | tf_op jit(solution)/shard_map/dot_general | solution.py:119
  (48 shorter events, 4.8 us)
Async XLA Ops:
  6.5 1.0 copy-start
  6.5 126.3 %all-reduce.2.cloned.1.call-start = ((), (), s32[]{:S(2)}) async-start(), calls=%async_computation.1 | async-start | bytes 262144 | tf_op jit(solution)/shard_map/psum | solution.py:50
  41.7 207.5 %reduce-scatter.2.cloned.1.call-start = ((), (), s32[]{:S(2)}) async-start(), calls=%async_computation.2 | async-start | bytes 1114112 | tf_op jit(solution)/shard_map/reduce_scatter | solution.py:79
  49.8 86.7 %copy-start.6 = (bf16[256,256]{1,0:T(8,128)(2,1)S(1)}, bf16[256,256]{1,0:T(8,128)(2,1)}, u32[]{:S(2)}) copy-start(bf16[256,256]{1,0:T(8,128)(2,1)} %param.9) | copy-start | bytes 393220
  132.8 3.7 %copy-start.2 = (bf16[8,1024,256]{2,1,0:T(8,128)(2,1)S(1)}, bf16[8,1024,256]{2,1,0:T(8,128)(2,1)}, u32[]{:S(2)}) copy-start(bf16[8,1024,256]{2,1,0:T(8,128)(2,1)} %param.7) | copy-start | bytes 12582916
  136.5 3.4 %copy-start.9 = (bf16[512,256]{1,0:T(8,128)(2,1)S(1)}, bf16[512,256]{1,0:T(8,128)(2,1)}, u32[]{:S(2)}) copy-start(bf16[512,256]{1,0:T(8,128)(2,1)} %param.11) | copy-start | bytes 786436
  136.5 3.4 %copy-start.10 = (bf16[256,512]{1,0:T(8,128)(2,1)S(1)}, bf16[256,512]{1,0:T(8,128)(2,1)}, u32[]{:S(2)}) copy-start(bf16[256,512]{1,0:T(8,128)(2,1)} %param.10) | copy-start | bytes 786436
  139.8 42.3 %copy-start.4 = (bf16[16,1024]{1,0:T(8,128)(2,1)S(1)}, bf16[16,1024]{1,0:T(8,128)(2,1)}, u32[]{:S(2)}) copy-start(bf16[16,1024]{1,0:T(8,128)(2,1)} %get-tuple-element.23) | copy-start | bytes 98308
  139.8 42.3 %copy-start.5 = (bf16[16,1024]{1,0:T(8,128)(2,1)S(1)}, bf16[16,1024]{1,0:T(8,128)(2,1)}, u32[]{:S(2)}) copy-start(bf16[16,1024]{1,0:T(8,128)(2,1)} %get-tuple-element.24) | copy-start | bytes 98308
  139.9 45.4 %copy-start.7 = (s32[8]{0:T(128)S(1)}, s32[8]{0:T(128)}, u32[]{:S(2)}) copy-start(s32[8]{0:T(128)} %iota_add_fusion) | copy-start | bytes 100
  139.9 45.4 %copy-start.8 = (s32[32]{0:T(128)S(1)}, s32[32]{0:T(128)}, u32[]{:S(2)}) copy-start(s32[32]{0:T(128)} %compare_select_fusion.1) | copy-start | bytes 388
  283.7 4.2 %copy-start.3 = (bf16[8192,256]{1,0:T(8,128)(2,1)S(1)}, bf16[8192,256]{1,0:T(8,128)(2,1)}, u32[]{:S(2)}) copy-start(bf16[8192,256]{1,0:T(8,128)(2,1)} %fusion.11) | copy-start | bytes 12582916
  283.7 4.2 %copy-start.11 = (bf16[256,256]{1,0:T(8,128)(2,1)S(1)}, bf16[256,256]{1,0:T(8,128)(2,1)}, u32[]{:S(2)}) copy-start(bf16[256,256]{1,0:T(8,128)(2,1)} %param.12) | copy-start | bytes 393220
  287.9 21.1 %copy-start.1 = (bf16[256,768]{1,0:T(8,128)(2,1)S(1)}, bf16[256,768]{1,0:T(8,128)(2,1)}, u32[]{:S(2)}) copy-start(bf16[256,768]{1,0:T(8,128)(2,1)} %param.8) | copy-start | bytes 1179652
Sparse Core Ops, SparseCore 0:
  41.8 90.9 all-reduce.1
  190.1 59.1 reduce-scatter.1
where the time goes:
time: 316 us
  waiting for transfers between devices  142 us (45%)
  matrix products  112 us (35%)
  blocking collectives  20.9 us (7%)
  other arithmetic  18.4 us (6%)
  between operations  13.7 us (4%)
  local copies, waits for them, and re-layouts  8.7 us (3%)
    psum x1, waiting for transfers between devices, local(): summed_kv = lax.psum(partial_kv, 'row')  83 us
    reduce_scatter x1, waiting for transfers between devices, local(): owned = lax.psum_scatter(term_modes, 'row', scatter_dimension=0, tiled=True)  59.1 us
    dot_general x1, matrix products, local(): jnp.dot(hidden, w_outer, preferred_element_type=jnp.float32)  42.3 us
    dot_general x1, matrix products, local(): skipped = jnp.dot(second, w_skip, preferred_element_type=jnp.float32)  21 us
    all_gather x1, blocking collectives, local(): segment = lax.all_gather(mixed, 'row', axis=0, tiled=True)  20.9 us
    dot_general x1, matrix products, local(): projected = jnp.dot(tokens, w_qkv, preferred_element_type=jnp.float32)  12.3 us
    dot_general x1, matrix products, local(): jnp.einsum('thd,the->hde', key_rows, value_rows, preferred_element_type=j...  7.98 us
    reduce_sum x1, other arithmetic, head_norm(): spread = jnp.mean(center * center, axis=-1, keepdims=True)  7.16 us
  transfers between devices with their start and end apart: 2, of which 2 were waited for; matrix products, arithmetic and copies ran while one was open for 3% of the time, Pallas kernels for 0%

commit v1 on v0

--- a/solution.py
+++ b/solution.py
@@ -47,7 +47,11 @@
     partial_kv = jnp.einsum(
         "thd,the->hde", key_rows, value_rows, preferred_element_type=jnp.float32
     )
-    summed_kv = lax.psum(partial_kv, "row")
+    summed_kv = partial_kv
+    for hop in (1, 2, 4, 8):
+        summed_kv = summed_kv + lax.ppermute(
+            summed_kv, "row", [(dev, dev ^ hop) for dev in range(16)]
+        )
     scaled_kv = (summed_kv / (height * columns)).astype(jnp.bfloat16)
     attended = jnp.einsum("thd,hde->the", queries, scaled_kv, preferred_element_type=jnp.float32)
     attended = attended.astype(jnp.bfloat16).reshape(-1, channels)

time: 316 us -> 250 us (0.79)
  waiting for transfers between devices: 142 us -> 69.7 us
  starting transfers between devices: 0.04 us -> 7.61 us
    psum x1 -> x0, waiting for transfers between devices: 83 us -> none  [local(): summed_kv = lax.psum(partial_kv, 'row')]
    ppermute x0 -> x4, waiting for transfers between devices: none -> 11.3 us  [local(): lax.ppermute(summed_kv, 'row', [(dev, dev ^ hop) for dev in range(16)])]
    ppermute x0 -> x4, starting transfers between devices: none -> 7.6 us  [local(): lax.ppermute(summed_kv, 'row', [(dev, dev ^ hop) for dev in range(16)])]
  transfers between devices with their start and end apart: 2 -> 5, of which waited for: 2 -> 4; matrix products, arithmetic and copies ran while one was open for 3% -> 3% of each run, Pallas kernels for 0% -> 0%
where the time goes in v1:
time: 250 us
  matrix products  111 us (44%)
  waiting for transfers between devices  69.7 us (28%)
  blocking collectives  20.8 us (8%)
  other arithmetic  18.3 us (7%)
  between operations  13.7 us (5%)
  local copies, waits for them, and re-layouts  8.7 us (3%)
  starting transfers between devices  7.61 us (3%)
    reduce_scatter x1, waiting for transfers between devices, local(): owned = lax.psum_scatter(term_modes, 'row', scatter_dimension=0, tiled=True)  58.3 us
    dot_general x1, matrix products, local(): jnp.dot(hidden, w_outer, preferred_element_type=jnp.float32)  42.3 us
    dot_general x1, matrix products, local(): skipped = jnp.dot(second, w_skip, preferred_element_type=jnp.float32)  21 us
    all_gather x1, blocking collectives, local(): segment = lax.all_gather(mixed, 'row', axis=0, tiled=True)  20.8 us
    dot_general x1, matrix products, local(): projected = jnp.dot(tokens, w_qkv, preferred_element_type=jnp.float32)  12.3 us
    ppermute x4, waiting for transfers between devices, local(): lax.ppermute(summed_kv, 'row', [(dev, dev ^ hop) for dev in range(16)])  11.3 us
    ppermute x4, starting transfers between devices, local(): lax.ppermute(summed_kv, 'row', [(dev, dev ^ hop) for dev in range(16)])  7.6 us
    dot_general x1, matrix products, local(): jnp.einsum('thd,the->hde', key_rows, value_rows, preferred_element_type=j...  7.26 us
  transfers between devices with their start and end apart: 5, of which 4 were waited for; matrix products, arithmetic and copies ran while one was open for 3% of the time, Pallas kernels for 0%

profile of v1, /device:TPU:0, one launch (start us, length us, event | category | flops | bytes accessed | tf_op | source)
XLA Modules:
  0.0 250.0 jit_solution(17334357402830248410)
XLA Ops:
  7.5 12.3 %fusion.165 = f32[8192,768]{0,1:T(8,128)} fusion(bf16[8192,256]{1,0:T(8,128)(2,1)} %bitcast.87, bf16[256,768]{1,0:T(8,128)(2,1)S(1)} %copy-done), kind=kOutput, calls=%fused_computation.221 | convolution fusion | flops 3221225472 | bytes 29753344 | tf_op jit(solution)/shard_map/dot_general | solution.py:43
  19.8 6.6 %bitcast_reduce_fusion.1 = (f32[8192,4]{0,1:T(4,128)S(1)}, f32[8192,4]{0,1:T(4,128)S(1)}) fusion(f32[8192,768]{0,1:T(8,128)} %fusion.165), kind=kLoop, calls=%fused_computation.37 | loop fusion | flops 4128768 | bytes 17039360 | tf_op jit(solution)/shard_map/reduce_sum | solution.py:16
  26.4 7.2 %multiply_reduce_fusion.1 = (f32[8192,4]{0,1:T(4,128)S(1)}, f32[8192,4]{0,1:T(4,128)S(1)}) fusion(f32[8192,768]{0,1:T(8,128)} %fusion.165, f32[8192,4]{0,1:T(4,128)S(1)} %get-tuple-element.22, f32[8192,4]{0,1:T(4,128)S(1)} %get-tuple-element.21), kind=kLoop, calls=%fused_computation.54 | loop fusion | flops 12517376 | bytes 17301504 | tf_op jit(solution)/shard_map/reduce_sum | solution.py:17
  33.7 7.3 %fusion.29 = f32[4,64,64]{2,1,0:T(8,128)S(1)} fusion(f32[8192,768]{0,1:T(8,128)} %fusion.165, f32[8192,4]{0,1:T(4,128)S(1)} %add_rsqrt_fusion, f32[8192,4]{0,1:T(4,128)S(1)} %get-tuple-element.21, f32[8192,4]{0,1:T(4,128)S(1)} %add_rsqrt_fusion.1, f32[8192,4]{0,1:T(4,128)S(1)} %get-tuple-element.22), kind=kOutput, calls=%fused_computation.58 | convolution fusion | flops 281018368 | bytes 17367040 | tf_op jit(solution)/shard_map/thd,the->hde/dot_general | solution.py:47
  41.5 6.0 %slice.91 = bf16[8192,256]{0,1:T(8,128)(2,1)} slice(f32[8192,768]{0,1:T(8,128)} %fusion.165), slice={[0:8192], [0:256]} | slice | bytes 8388608 | tf_op jit(solution)/shard_map/slice | solution.py:44
  47.5 2.6 %collective-permute-start.1 = (f32[4,64,64]{2,1,0:T(8,128)S(1)}, f32[4,64,64]{2,1,0:T(8,128)S(1)}, u32[]{:S(2)}, u32[]{:S(2)}) collective-permute-start(f32[4,64,64]{2,1,0:T(8,128)S(1)} %add.130), channel_id=1, source_target_pairs={{0,2},{1,3},{2,0},{3,1},{4,6},{5,7},{6,4},{7,5},{8,10},{9,11},{10,... | collective-permute-start | bytes 196616 | tf_op jit(solution)/shard_map/ppermute | solution.py:52
  51.0 3.3 %collective-permute-done.1 = f32[4,64,64]{2,1,0:T(8,128)S(1)} collective-permute-done((f32[4,64,64]{2,1,0:T(8,128)S(1)}, f32[4,64,64]{2,1,0:T(8,128)S(1)}, u32[]{:S(2)}, u32[]{:S(2)}) %collective-permute-start.1) | collective-permute-done | bytes 65568 | tf_op jit(solution)/shard_map/ppermute | solution.py:52
  54.3 1.9 collective-permute-start.2
  56.7 3.0 %collective-permute-done.2 = f32[4,64,64]{2,1,0:T(8,128)S(1)} collective-permute-done((f32[4,64,64]{2,1,0:T(8,128)S(1)}, f32[4,64,64]{2,1,0:T(8,128)S(1)}, u32[]{:S(2)}, u32[]{:S(2)}) %collective-permute-start.2) | collective-permute-done | bytes 65568 | tf_op jit(solution)/shard_map/ppermute | solution.py:52
  59.7 2.6 %collective-permute-start.3 = (f32[4,64,64]{2,1,0:T(8,128)S(1)}, f32[4,64,64]{2,1,0:T(8,128)S(1)}, u32[]{:S(2)}, u32[]{:S(2)}) collective-permute-start(f32[4,64,64]{2,1,0:T(8,128)S(1)} %add.132), channel_id=1, source_target_pairs={{0,8},{1,9},{2,10},{3,11},{4,12},{5,13},{6,14},{7,15},{8,0},{9,1},... | collective-permute-start | bytes 196616 | tf_op jit(solution)/shard_map/ppermute | solution.py:52
  62.8 5.1 %collective-permute-done.3 = f32[4,64,64]{2,1,0:T(8,128)S(1)} collective-permute-done((f32[4,64,64]{2,1,0:T(8,128)S(1)}, f32[4,64,64]{2,1,0:T(8,128)S(1)}, u32[]{:S(2)}, u32[]{:S(2)}) %collective-permute-start.3) | collective-permute-done | bytes 65568 | tf_op jit(solution)/shard_map/ppermute | solution.py:52
  67.9 3.5 %convolution_convert_fusion = bf16[4,64,8192]{2,1,0:T(8,128)(2,1)S(1)} fusion(bf16[8192,4,64]{0,2,1:T(8,128)(2,1)} %bitcast.86, f32[4,64,64]{2,1,0:T(8,128)S(1)} %add.132, f32[4,64,64]{2,1,0:T(8,128)S(1)} %collective-permute-done.3), kind=kOutput, calls=%fused_computation.22 | convolution fusion | flops 270581760 | bytes 8519680 | tf_op jit(solution)/shard_map/thd,hde->the/dot_general | solution.py:56
  71.5 3.3 %fusion.10 = bf16[8192,256]{1,0:T(8,128)(2,1)} fusion(bf16[8192,256]{0,1:T(8,128)(2,1)S(1)} %bitcast.85, bf16[256,256]{1,0:T(8,128)(2,1)S(1)} %copy-done.6, bf16[8192,256]{1,0:T(8,128)(2,1)S(1)} %bitcast.88), kind=kOutput, calls=%fused_computation.23 | convolution fusion | flops 1080033280 | bytes 12713984 | tf_op jit(solution)/shard_map/dot_general | solution.py:59
  74.8 42.3 %fusion.11 = bf16[8192,256]{1,0:T(8,128)(2,1)} fusion(bf16[512,256]{1,0:T(8,128)(2,1)S(1)} %copy-done.9, bf16[8192,256]{1,0:T(8,128)(2,1)} %fusion.10, bf16[256,512]{1,0:T(8,128)(2,1)S(1)} %copy-done.10), kind=kOutput, calls=%fused_computation.25 | convolution fusion | flops 4573888512 | bytes 8912896 | tf_op jit(solution)/shard_map/dot_general | solution.py:65
  117.1 3.0 %convolution_bitcast_fusion = f32[8,32,256]{2,1,0:T(8,128)S(1)} fusion(bf16[8,1024,256]{2,1,0:T(8,128)(2,1)} %bitcast.90, bf16[16,1024]{1,0:T(8,128)(2,1)S(1)} %copy-done.4, bf16[16,1024]{1,0:T(8,128)(2,1)S(1)} %copy-done.5), kind=kOutput, calls=%fused_computation.79 | convolution fusion | flops 134348800 | bytes 4521984 | tf_op jit(solution)/shard_map/rwc,wk->rkc/dot_general | solution.py:70
  123.3 1.6 copy.18
  125.1 58.3 %reduce-scatter.2.cloned.1.call-done = f32[32,512]{1,0:T(8,128)} async-done(((f32[512,512]{1,0:T(8,128)}), f32[32,512]{1,0:T(8,128)}) %reduce-scatter.2.cloned.1.call-update) | async-done | bytes 65552 | tf_op jit(solution)/shard_map/reduce_scatter | solution.py:83
  184.3 2.8 %fusion.30 = f32[32,1,256]{2,1,0:T(1,128)S(1)} fusion(bf16[32,2,256,256]{3,2,1,0:T(8,128)(2,1)} %param.13, bf16[32,256,1]{1,0,2:T(8,128)(2,1)S(1)} %get-tuple-element.17), kind=kOutput, calls=%fused_computation.59 | convolution fusion | flops 4194304 | bytes 4243456 | tf_op jit(solution)/shard_map/mc,mco->mo/dot_general | solution.py:92
  187.1 2.8 %fusion.36 = f32[32,1,256]{2,1,0:T(1,128)S(1)} fusion(bf16[32,2,256,256]{3,2,1,0:T(8,128)(2,1)} %param.13, bf16[32,256,1]{1,0,2:T(8,128)(2,1)S(1)} %get-tuple-element.17), kind=kOutput, calls=%fused_computation.65 | convolution fusion | flops 4194304 | bytes 4243456 | tf_op jit(solution)/shard_map/mc,mco->mo/dot_general | solution.py:89
  190.0 2.8 %fusion.34 = f32[32,1,256]{2,1,0:T(1,128)S(1)} fusion(bf16[32,2,256,256]{3,2,1,0:T(8,128)(2,1)} %param.13, bf16[32,256,1]{1,0,2:T(8,128)(2,1)S(1)} %get-tuple-element.18), kind=kOutput, calls=%fused_computation.63 | convolution fusion | flops 4194304 | bytes 4243456 | tf_op jit(solution)/shard_map/mc,mco->mo/dot_general | solution.py:94
  192.8 2.8 %fusion.32 = f32[32,1,256]{2,1,0:T(1,128)S(1)} fusion(bf16[32,2,256,256]{3,2,1,0:T(8,128)(2,1)} %param.13, bf16[32,256,1]{1,0,2:T(8,128)(2,1)S(1)} %get-tuple-element.18), kind=kOutput, calls=%fused_computation.61 | convolution fusion | flops 4194304 | bytes 4243456 | tf_op jit(solution)/shard_map/mc,mco->mo/dot_general | solution.py:91
  195.7 20.8 %all_gather.3 = bf16[512,512]{1,0:T(8,128)(2,1)S(1)} all-gather(bf16[32,512]{1,0:T(8,128)(2,1)S(1)} %pad_maximum_fusion.1), channel_id=1, replica_groups=mesh['grp'=2,'row'=16] {'row'}, dimensions={0}, use_global_device_ids=true | all-gather | bytes 557056 | tf_op jit(solution)/shard_map/all_gather | solution.py:96
  217.9 2.8 %fusion.52 = bf16[8,16,512]{2,1,0:T(8,128)(2,1)S(1)} fusion(f32[512,8,256]{2,0,1:T(8,128)S(1)} %get-tuple-element.10, f32[512,8,256]{2,0,1:T(8,128)S(1)} %get-tuple-element.9, f32[16]{0:T(128)S(1)} %fusion.110, s32[512]{0:T(512)S(1)} %fusion.97), kind=kOutput, calls=%fused_computation.82 | convolution fusion | flops 404889600 | bytes 8521792 | tf_op jit(solution)/shard_map/mk,mrc->rkc/dot_general | solution.py:113
  222.1 21.0 %fusion.14 = bf16[8192,256]{1,0:T(8,128)(2,1)} fusion(f32[8192,256]{1,0:T(8,128)S(1)} %bitcast.89, bf16[8192,256]{1,0:T(8,128)(2,1)S(1)} %copy-done.3, bf16[256,256]{1,0:T(8,128)(2,1)S(1)} %copy-done.11), kind=kOutput, calls=%fused_computation.28 | convolution fusion | flops 1212153856 | bytes 16908288 | tf_op jit(solution)/shard_map/dot_general | solution.py:123
  (56 shorter events, 10.6 us)
Async XLA Ops:
  6.5 1.0 copy-start
  6.5 176.9 %reduce-scatter.2.cloned.1.call-start = ((), (), s32[]{:S(2)}) async-start(), calls=%async_computation.1 | async-start | bytes 1114112 | tf_op jit(solution)/shard_map/reduce_scatter | solution.py:83
  41.0 6.5 %collective-permute-start = (f32[4,64,64]{2,1,0:T(8,128)S(1)}, f32[4,64,64]{2,1,0:T(8,128)S(1)}, u32[]{:S(2)}, u32[]{:S(2)}) collective-permute-start(f32[4,64,64]{2,1,0:T(8,128)S(1)} %fusion.29), channel_id=1, source_target_pairs={{0,1},{1,0},{2,3},{3,2},{4,5},{5,4},{6,7},{7,6},{8,9},{9,8},{10,11... | collective-permute-start | bytes 196616 | tf_op jit(solution)/shard_map/ppermute | solution.py:52
  47.5 23.9 %copy-start.6 = (bf16[256,256]{1,0:T(8,128)(2,1)S(1)}, bf16[256,256]{1,0:T(8,128)(2,1)}, u32[]{:S(2)}) copy-start(bf16[256,256]{1,0:T(8,128)(2,1)} %param.9) | copy-start | bytes 393220
  47.5 23.9 %copy-start.2 = (bf16[8,1024,256]{2,1,0:T(8,128)(2,1)S(1)}, bf16[8,1024,256]{2,1,0:T(8,128)(2,1)}, u32[]{:S(2)}) copy-start(bf16[8,1024,256]{2,1,0:T(8,128)(2,1)} %param.7) | copy-start | bytes 12582916
  47.5 6.7 %collective-permute-start.1 = (f32[4,64,64]{2,1,0:T(8,128)S(1)}, f32[4,64,64]{2,1,0:T(8,128)S(1)}, u32[]{:S(2)}, u32[]{:S(2)}) collective-permute-start(f32[4,64,64]{2,1,0:T(8,128)S(1)} %add.130), channel_id=1, source_target_pairs={{0,2},{1,3},{2,0},{3,1},{4,6},{5,7},{6,4},{7,5},{8,10},{9,11},{10,... | collective-permute-start | bytes 196616 | tf_op jit(solution)/shard_map/ppermute | solution.py:52
  54.3 5.4 %collective-permute-start.2 = (f32[4,64,64]{2,1,0:T(8,128)S(1)}, f32[4,64,64]{2,1,0:T(8,128)S(1)}, u32[]{:S(2)}, u32[]{:S(2)}) collective-permute-start(f32[4,64,64]{2,1,0:T(8,128)S(1)} %add.131), channel_id=1, source_target_pairs={{0,4},{1,5},{2,6},{3,7},{4,0},{5,1},{6,2},{7,3},{8,12},{9,13},{10,... | collective-permute-start | bytes 196616 | tf_op jit(solution)/shard_map/ppermute | solution.py:52
  59.7 8.2 %collective-permute-start.3 = (f32[4,64,64]{2,1,0:T(8,128)S(1)}, f32[4,64,64]{2,1,0:T(8,128)S(1)}, u32[]{:S(2)}, u32[]{:S(2)}) collective-permute-start(f32[4,64,64]{2,1,0:T(8,128)S(1)} %add.132), channel_id=1, source_target_pairs={{0,8},{1,9},{2,10},{3,11},{4,12},{5,13},{6,14},{7,15},{8,0},{9,1},... | collective-permute-start | bytes 196616 | tf_op jit(solution)/shard_map/ppermute | solution.py:52
  71.4 3.4 %copy-start.9 = (bf16[512,256]{1,0:T(8,128)(2,1)S(1)}, bf16[512,256]{1,0:T(8,128)(2,1)}, u32[]{:S(2)}) copy-start(bf16[512,256]{1,0:T(8,128)(2,1)} %param.11) | copy-start | bytes 786436
  71.4 3.4 %copy-start.10 = (bf16[256,512]{1,0:T(8,128)(2,1)S(1)}, bf16[256,512]{1,0:T(8,128)(2,1)}, u32[]{:S(2)}) copy-start(bf16[256,512]{1,0:T(8,128)(2,1)} %param.10) | copy-start | bytes 786436
  74.8 42.3 %copy-start.4 = (bf16[16,1024]{1,0:T(8,128)(2,1)S(1)}, bf16[16,1024]{1,0:T(8,128)(2,1)}, u32[]{:S(2)}) copy-start(bf16[16,1024]{1,0:T(8,128)(2,1)} %get-tuple-element.23) | copy-start | bytes 98308
  74.8 42.3 %copy-start.5 = (bf16[16,1024]{1,0:T(8,128)(2,1)S(1)}, bf16[16,1024]{1,0:T(8,128)(2,1)}, u32[]{:S(2)}) copy-start(bf16[16,1024]{1,0:T(8,128)(2,1)} %get-tuple-element.24) | copy-start | bytes 98308
  74.8 45.4 %copy-start.7 = (s32[8]{0:T(128)S(1)}, s32[8]{0:T(128)}, u32[]{:S(2)}) copy-start(s32[8]{0:T(128)} %iota_add_fusion) | copy-start | bytes 100
  74.8 45.4 %copy-start.8 = (s32[32]{0:T(128)S(1)}, s32[32]{0:T(128)}, u32[]{:S(2)}) copy-start(s32[32]{0:T(128)} %compare_select_fusion.1) | copy-start | bytes 388
  217.9 4.2 %copy-start.3 = (bf16[8192,256]{1,0:T(8,128)(2,1)S(1)}, bf16[8192,256]{1,0:T(8,128)(2,1)}, u32[]{:S(2)}) copy-start(bf16[8192,256]{1,0:T(8,128)(2,1)} %fusion.11) | copy-start | bytes 12582916
  217.9 4.2 %copy-start.11 = (bf16[256,256]{1,0:T(8,128)(2,1)S(1)}, bf16[256,256]{1,0:T(8,128)(2,1)}, u32[]{:S(2)}) copy-start(bf16[256,256]{1,0:T(8,128)(2,1)} %param.12) | copy-start | bytes 393220
  222.1 21.1 %copy-start.1 = (bf16[256,768]{1,0:T(8,128)(2,1)S(1)}, bf16[256,768]{1,0:T(8,128)(2,1)}, u32[]{:S(2)}) copy-start(bf16[256,768]{1,0:T(8,128)(2,1)} %param.8) | copy-start | bytes 1179652
Sparse Core Ops, SparseCore 0:
  125.0 58.3 reduce-scatter.1
